TPU v7x, 256 devices: a whole 4x4x8 slice. The times are simulated.
256 devices in a mesh: seq: 32 (over z, x), head: 8 (over y, core).
Axes of the slice: x: 4, y: 4, z: 8, core: 2. Of those that a mesh axis runs over, the one named last changes fastest.
Arguments:
- block_input: bfloat16 [8, 256, 5120], P(None, 'seq'), may hold values from -6 to 6
- accepted: bfloat16 [8, 256, 5120], P(None, 'seq'), may hold values from -6 to 6
- accept_mask: int32 [8, 256], P(None, 'seq'), may hold values 0 or 1
- cache_lengths: int32 [8], replicated, may hold values from 1 to 8192, as said below
- page_table: int32 [512], replicated, may hold values from 0 to 511, each once
- norm_gain: float32 [5120], replicated, may hold values from 0.1 to 1.9
- w_query: bfloat16 [5120, 3072], P('seq', 'head'), may hold values from -0.078125 to 0.078125
- w_key: bfloat16 [5120, 3072], P('seq', 'head'), may hold values from -0.078125 to 0.078125
- w_value: bfloat16 [5120, 3072], P('seq', 'head'), may hold values from -0.25 to 0.25
- w_out: bfloat16 [5120, 3072], P('seq', 'head'), may hold values from -0.109375 to 0.109375
- key_cache: bfloat16 [512, 128, 3072], P('seq', None, 'head')
- value_cache: bfloat16 [512, 128, 3072], P('seq', None, 'head'), may hold values from -18 to 18
Outputs:
- first_out: bfloat16 [8, 256, 5120], P(None, 'seq', 'head')
- second_out: bfloat16 [8, 256, 5120], P(None, 'seq', 'head')
Inputs may be any that keep to these rules, and one draw needn't show every extreme that they name: `cache_lengths`: max(1, 4) requests, chosen at random, hold (63) * 128 + 1 to 8192 cached tokens, one of them exactly 8192; the others hold 1 to 256. `page_table`: A permutation of the 512 pool pages; entry r * 64 + j is the pool page of cached positions j * 128 to (j + 1) * 128 - 1 of request r.
All inputs are finite; a program needn't handle non-finite values. No bound on the sum of `accept_mask` on one device may be relied on, other than what follows from the above.
Results may differ from a plain program's by a relative error of at most 0.024.
The roundings to bfloat16 on the way count: a program that leaves them out, or rounds other values in their place, can miss the bound.
Values may be sent and summed in bfloat16 or wider, within the bound.
A program may use at most 128 MiB of HBM per device.

v0:
```python
import jax
import jax.numpy as jnp
from jax import lax
from jax.sharding import PartitionSpec as P

HD = 128
PAGE = 128
MAXP = 64
masked_score = -1e30


def rotate(vectors, positions):
    half_width = vectors.shape[-1] // 2
    frequency = 10000.0 ** (-(jnp.arange(half_width).astype(jnp.float32) * 2.0) / vectors.shape[-1])
    angles = positions[..., None, None] * frequency
    cosine = jnp.cos(angles)
    sine_part = jnp.sin(angles)
    front_half = vectors[..., :half_width]
    back_half = vectors[..., half_width:]
    return jnp.concatenate(
        [front_half * cosine - back_half * sine_part, back_half * cosine + front_half * sine_part],
        axis=-1,
    )


def normalize(inputs, norm_gain):
    widened = inputs.astype(jnp.float32)
    inverse = lax.rsqrt(jnp.mean(widened * widened, axis=-1, keepdims=True) + 1e-05)
    return (widened * inverse * norm_gain).astype(jnp.bfloat16)


def per_device(
    block_input,
    accepted,
    accept_mask,
    cache_lengths,
    page_table,
    norm_gain,
    w_query,
    w_key,
    w_value,
    w_out,
    key_cache,
    value_cache,
):
    seq_place = lax.axis_index("seq")
    requests, part_len, model_width = block_input.shape
    local_width = w_query.shape[1]
    local_heads = local_width // HD
    row_count = 2 * requests * part_len
    swapped = jnp.where(accept_mask[:, :, None] == 1, accepted, block_input)
    token_rows = normalize(jnp.stack([block_input, swapped]), norm_gain).reshape(
        row_count, model_width
    )
    full_query, full_key, full_value, out_weight = (
        lax.all_gather(w_query, "seq", axis=0, tiled=True),
        lax.all_gather(w_key, "seq", axis=0, tiled=True),
        lax.all_gather(w_value, "seq", axis=0, tiled=True),
        lax.all_gather(w_out, "seq", axis=0, tiled=True),
    )
    query_rows = jnp.dot(token_rows, full_query, preferred_element_type=jnp.float32)
    key_rows = jnp.dot(token_rows, full_key, preferred_element_type=jnp.float32)
    value_rows = jnp.dot(token_rows, full_value, preferred_element_type=jnp.float32)
    positions = (
        cache_lengths[:, None]
        + seq_place * part_len
        + jnp.arange(part_len, dtype=jnp.int32)[None, :]
    ).astype(jnp.float32)
    shaped = (2, requests, part_len, local_heads, HD)
    new_queries = rotate(query_rows.reshape(shaped), positions).astype(jnp.bfloat16)
    new_keys = rotate(key_rows.reshape(shaped), positions).astype(jnp.bfloat16)
    new_values = value_rows.reshape(shaped).astype(jnp.bfloat16)
    every_query = lax.all_gather(new_queries, "seq", axis=2, tiled=True)
    pages_here = key_cache.shape[0]
    page_ids = seq_place * pages_here + jnp.arange(pages_here, dtype=jnp.int32)
    table_slots = jnp.arange(page_table.shape[0], dtype=jnp.int32)
    slot_of = jnp.sum(
        jnp.where(page_table[None, :] == page_ids[:, None], table_slots[None, :], 0), axis=1
    )
    page_owner = slot_of // MAXP
    owner_match = page_owner[:, None] == jnp.arange(requests, dtype=jnp.int32)[None, :]
    owner_length = jnp.sum(jnp.where(owner_match, cache_lengths[None, :], 0), axis=1)
    offsets = (slot_of % MAXP)[:, None] * PAGE + jnp.arange(PAGE, dtype=jnp.int32)[None, :]
    live_mask = (offsets < owner_length[:, None])[:, None, None, :]
    owner_hot = owner_match.astype(jnp.float32)
    cached_keys = key_cache.reshape(pages_here, PAGE, local_heads, HD)
    cached_values = value_cache.reshape(pages_here, PAGE, local_heads, HD)
    score_scale = HD ** (-0.5)

    def local_part(pass_items):
        pass_queries, pass_keys, pass_values = pass_items
        page_queries = jnp.take(pass_queries, page_owner, axis=0)
        scores = (
            jnp.einsum(
                "pqhd,pkhd->pqhk", page_queries, cached_keys, preferred_element_type=jnp.float32
            )
            * score_scale
        )
        scores = jnp.where(live_mask, scores, masked_score)
        page_peak = jnp.max(scores, axis=-1)
        weights = jnp.where(live_mask, jnp.exp(scores - page_peak[..., None]), 0.0)
        page_total = jnp.sum(weights, axis=-1)
        page_out = jnp.einsum(
            "pqhk,pkhd->pqhd",
            weights.astype(jnp.bfloat16),
            cached_values,
            preferred_element_type=jnp.float32,
        )
        owner_peak = jnp.max(
            jnp.where(owner_match[:, :, None, None], page_peak[:, None], masked_score), axis=0
        )
        factor = jnp.exp(page_peak - jnp.take(owner_peak, page_owner, axis=0))
        cache_total = jnp.einsum(
            "pr,pqh->rqh", owner_hot, page_total * factor, precision=lax.Precision.HIGHEST
        )
        cache_out = jnp.einsum(
            "pr,pqhd->rqhd",
            owner_hot,
            page_out * factor[..., None],
            precision=lax.Precision.HIGHEST,
        )
        block_scores = (
            jnp.einsum(
                "rqhd,rkhd->rqhk", pass_queries, pass_keys, preferred_element_type=jnp.float32
            )
            * score_scale
        )
        block_peak = jnp.max(block_scores, axis=-1)
        block_weights = jnp.exp(block_scores - block_peak[..., None])
        block_total = jnp.sum(block_weights, axis=-1)
        block_out = jnp.einsum(
            "rqhk,rkhd->rqhd",
            block_weights,
            pass_values.astype(jnp.float32),
            precision=lax.Precision.HIGHEST,
        )
        row_peak = jnp.maximum(owner_peak, block_peak)
        cache_factor = jnp.exp(owner_peak - row_peak)
        block_factor = jnp.exp(block_peak - row_peak)
        joined_total = cache_total * cache_factor + block_total * block_factor
        joined_out = cache_out * cache_factor[..., None] + block_out * block_factor[..., None]
        return (row_peak, joined_total, joined_out)

    row_peak, row_total, row_out = lax.map(local_part, (every_query, new_keys, new_values))
    overall = lax.pmax(row_peak, "seq")
    rescale = jnp.exp(row_peak - overall)
    summed_out, summed_total = (
        lax.psum_scatter(row_out * rescale[..., None], "seq", scatter_dimension=2, tiled=True),
        lax.psum_scatter(row_total * rescale, "seq", scatter_dimension=2, tiled=True),
    )
    context = (
        (summed_out / summed_total[..., None]).astype(jnp.bfloat16).reshape(row_count, local_width)
    )
    partial_value = lax.dot_general(
        context, out_weight, (((1,), (1,)), ((), ())), preferred_element_type=jnp.float32
    )
    own_share = lax.psum_scatter(partial_value, "head", scatter_dimension=1, tiled=True).astype(
        jnp.bfloat16
    )
    result = own_share.reshape(2, requests, part_len, own_share.shape[1])
    return (result[0], result[1])


def solution(mesh):
    placed = (
        P(None, "seq", None),
        P(None, "seq", None),
        P(None, "seq"),
        P(),
        P(),
        P(),
        P("seq", "head"),
        P("seq", "head"),
        P("seq", "head"),
        P("seq", "head"),
        P("seq", None, "head"),
        P("seq", None, "head"),
    )
    return jax.shard_map(
        per_device,
        mesh=mesh,
        in_specs=placed,
        out_specs=(P(None, "seq", "head"), P(None, "seq", "head")),
        check_vma=False,
    )
```

profile of v0, /device:TPU:2, one launch (start us, length us, event | category | flops | bytes accessed | tf_op | source)
XLA Modules:
  0.0 919.2 jit_solution(8133665721481068145)
XLA Ops:
  13.3 80.1 %all-gather.10.cloned.1.call-done = bf16[5120,384]{1,0:T(8,128)(2,1)} async-done(((bf16[160,384]{1,0:T(8,128)(2,1)}), bf16[5120,384]{1,0:T(8,128)(2,1)}) %all-gather.10.cloned.1.call-update) | async-done | bytes 3932176 | tf_op jit(solution)/shard_map/all_gather | solution.py:57
  93.4 6.3 copy.77
  99.7 74.6 %all-gather.6.cloned.1.call-done = bf16[5120,384]{1,0:T(8,128)(2,1)} async-done(((bf16[160,384]{1,0:T(8,128)(2,1)}), bf16[5120,384]{1,0:T(8,128)(2,1)}) %all-gather.6.cloned.1.call-update) | async-done | bytes 3932176 | tf_op jit(solution)/shard_map/all_gather | solution.py:56
  174.3 6.3 copy.75
  180.6 3.5 fusion.59
  193.9 61.3 %all-gather.12.cloned.1.call-done = bf16[5120,384]{1,0:T(8,128)(2,1)} async-done(((bf16[160,384]{1,0:T(8,128)(2,1)}), bf16[5120,384]{1,0:T(8,128)(2,1)}) %all-gather.12.cloned.1.call-update) | async-done | bytes 3932176 | tf_op jit(solution)/shard_map/all_gather | solution.py:58
  255.2 6.3 copy.79
  262.2 4.0 convolution_convert_fusion
  266.2 69.3 %all-gather.8.cloned.1.call-done = bf16[2,8,256,3,128]{4,2,3,1,0:T(8,128)(2,1)} async-done(((bf16[2,8,8,3,128]{4,2,3,1,0:T(8,128)(2,1)}), bf16[2,8,256,3,128]{4,2,3,1,0:T(8,128)(2,1)}) %all-gather.8.cloned.1.call-update) | async-done | bytes 3145744 | tf_op jit(solution)/shard_map/all_gather | solution.py:73
  335.5 82.3 %while.16 = (s32[]{:T(128)}, f32[2,8,256,3]{2,1,3,0:T(8,128)}, f32[2,8,256,3]{2,1,3,0:T(8,128)}, f32[2,8,256,3,128]{4,2,3,1,0:T(8,128)}, s32[16]{0:T(128)S(1)}, ...) while((s32[]{:T(128)}, f32[2,8,256,3]{2,1,3,0:T(8,128)}, ...), condition=%wide.region_9.10_spmd.clone.clone, body=%wide.region_3.9_spmd.clone.clone.sunk | while | flops 1071998720 | bytes 124305208 | solution.py:144
  337.0 2.7 gather_fusion
  339.8 3.0 bitcast_reduce_fusion.2
  346.8 8.2 bitcast_multiply_fusion.4
  362.2 11.2 %fusion.103 = f32[1,8,256,3,128]{4,1,3,2,0:T(8,128)S(1)} fusion(f32[8,3,128,256]{2,0,1,3:T(8,128)} %copy.126, f32[16,256,3,128]{3,1,2,0:T(8,128)} %bitcast_multiply_fusion.4, f32[8,256,3]{0,2,1:T(4,128)} %copy.127, f32[8,256,3]{0,2,1:T(4,128)} %copy.128, s32[16]{0:T(128)S(1)} %get-tuple-element.340), kind=kOutput, calls=%fused_computation.19.clone.1 | convolution fusion | flops 153354496 | bytes 12632128 | tf_op jit(solution)/shard_map/while/body/eval_jaxpr/pr,pqhd->rqhd/dot_general | solution.py:116
  380.9 3.0 bitcast_reduce_fusion.2
  387.9 8.2 bitcast_multiply_fusion.4
  403.4 11.2 %fusion.103 = f32[1,8,256,3,128]{4,1,3,2,0:T(8,128)S(1)} fusion(f32[8,3,128,256]{2,0,1,3:T(8,128)} %copy.126, f32[16,256,3,128]{3,1,2,0:T(8,128)} %bitcast_multiply_fusion.4, f32[8,256,3]{0,2,1:T(4,128)} %copy.127, f32[8,256,3]{0,2,1:T(4,128)} %copy.128, s32[16]{0:T(128)S(1)} %get-tuple-element.340), kind=kOutput, calls=%fused_computation.19.clone.1 | convolution fusion | flops 153354496 | bytes 12632128 | tf_op jit(solution)/shard_map/while/body/eval_jaxpr/pr,pqhd->rqhd/dot_general | solution.py:116
  417.8 137.8 %pmax.7 = f32[2,8,256,3]{2,1,3,0:T(8,128)S(1)} all-reduce(f32[2,8,256,3]{2,1,3,0:T(8,128)} %get-tuple-element.72), channel_id=1, replica_groups=mesh['seq'=32,'head'=8] {'seq'}, use_global_device_ids=true, to_apply=%region_10.11 | all-reduce | flops 12288 | bytes 98304 | tf_op jit(solution)/shard_map/pmax | solution.py:145
  556.5 7.3 broadcast_multiply_fusion
  565.7 140.1 %all-reduce = f32[2,8,256,3]{2,1,3,0:T(8,128)S(1)} all-reduce(f32[2,8,256,3]{2,1,3,0:T(8,128)S(1)} %get-tuple-element.201), channel_id=3, replica_groups=mesh['seq'=32,'head'=8] {'seq'}, use_global_device_ids=true, to_apply=%region_12.13.clone | all-reduce | flops 12288 | bytes 98304
  706.0 82.0 %reduce-scatter.4.cloned.1.call-done = f32[2,8,8,3,128]{4,2,3,1,0:T(8,128)} async-done(((f32[2,8,256,3,128]{4,2,3,1,0:T(8,128)}), f32[2,8,8,3,128]{4,2,3,1,0:T(8,128)}) %reduce-scatter.4.cloned.1.call-update) | async-done | bytes 196624 | tf_op jit(solution)/shard_map/reduce_scatter | solution.py:148
  789.1 80.8 %all-gather.14.cloned.1.call-done = bf16[5120,384]{1,0:T(8,128)(2,1)} async-done(((bf16[160,384]{1,0:T(8,128)(2,1)}), bf16[5120,384]{1,0:T(8,128)(2,1)}) %all-gather.14.cloned.1.call-update) | async-done | bytes 3932176 | tf_op jit(solution)/shard_map/all_gather | solution.py:59
  869.8 5.0 fusion.66
  874.8 35.8 %reduce-scatter.6.cloned.1.call-done = f32[128,640]{1,0:T(8,128)} async-done(((f32[128,5120]{1,0:T(8,128)}), f32[128,640]{1,0:T(8,128)}) %reduce-scatter.6.cloned.1.call-update) | async-done | bytes 327696 | tf_op jit(solution)/shard_map/reduce_scatter | solution.py:157
  (136 shorter events, 55.7 us)
Async XLA Ops:
  7.2 5.8 copy-start.13
  7.2 86.2 %all-gather.10.cloned.1.call-start = ((), (), s32[]{:S(2)}) async-start(), calls=%async_computation.4 | async-start | bytes 4055040 | tf_op jit(solution)/shard_map/all_gather | solution.py:57
  7.9 166.4 %all-gather.6.cloned.1.call-start = ((), (), s32[]{:S(2)}) async-start(), calls=%async_computation.2 | async-start | bytes 4055040 | tf_op jit(solution)/shard_map/all_gather | solution.py:56
  8.7 246.5 %all-gather.12.cloned.1.call-start = ((), (), s32[]{:S(2)}) async-start(), calls=%async_computation.5 | async-start | bytes 4055040 | tf_op jit(solution)/shard_map/all_gather | solution.py:58
  9.4 326.1 %all-gather.8.cloned.1.call-start = ((), (), s32[]{:S(2)}) async-start(), calls=%async_computation.3 | async-start | bytes 3244032 | tf_op jit(solution)/shard_map/all_gather | solution.py:73
  174.3 6.3 copy-start.3
  174.3 6.3 copy-start.12
  180.6 3.5 copy-start.2
  186.4 601.6 %reduce-scatter.4.cloned.1.call-start = ((), (), s32[]{:S(2)}) async-start(), calls=%async_computation.6 | async-start | bytes 6488064 | tf_op jit(solution)/shard_map/reduce_scatter | solution.py:148
  190.0 3.6 copy-start.11
  337.0 2.8 copy-start.4
  342.8 2.6 copy-start
  346.8 8.2 copy-start.1
  346.8 8.2 copy-start.6
  373.4 2.3 copy-start.9
  373.4 2.5 copy-start.7
  378.2 2.8 copy-start.4
  383.9 2.6 copy-start
  387.9 8.3 copy-start.1
  387.9 8.3 copy-start.6
  414.6 2.4 copy-start.9
  414.6 2.6 copy-start.7
  563.9 306.0 %all-gather.14.cloned.1.call-start = ((), (), s32[]{:S(2)}) async-start(), calls=%async_computation.7 | async-start | bytes 4055040 | tf_op jit(solution)/shard_map/all_gather | solution.py:59
  564.4 346.2 %reduce-scatter.6.cloned.1.call-start = ((), (), s32[]{:S(2)}) async-start(), calls=%async_computation.8 | async-start | bytes 2949120 | tf_op jit(solution)/shard_map/reduce_scatter | solution.py:157
  (7 other events, 6.0 us)
Sparse Core Ops, SparseCore 0:
  10.6 82.7 all-gather.9
  96.0 78.2 all-gather.5
  176.9 78.2 all-gather.11
  257.5 77.9 all-gather.7
  564.0 223.9 reduce-scatter.3
  790.8 79.0 all-gather.13
  874.9 35.6 reduce-scatter.5
where the time goes:
time: 920 us; the launch traced here: 919 us
  waiting for transfers between devices  487 us (53%)
  blocking collectives  278 us (30%)
  matrix products  64.6 us (7%)
  local copies, waits for them, and re-layouts  53.1 us (6%)
  other arithmetic  21.4 us (2%)
  between operations  14.9 us (2%)
    unnamed x1, blocking collectives  140 us
    pmax x1, blocking collectives, per_device(): overall = lax.pmax(row_peak, 'seq')  138 us
    reduce_scatter x1, waiting for transfers between devices, per_device(): lax.psum_scatter(row_out * rescale[..., None], 'seq', scatter_dimension=2...  82 us
    all_gather x1, waiting for transfers between devices, per_device(): lax.all_gather(w_out, 'seq', axis=0, tiled=True)  80.8 us
    all_gather x1, waiting for transfers between devices, per_device(): lax.all_gather(w_key, 'seq', axis=0, tiled=True)  80.1 us
    all_gather x1, waiting for transfers between devices, per_device(): lax.all_gather(w_query, 'seq', axis=0, tiled=True)  74.6 us
    all_gather x1, waiting for transfers between devices, per_device(): every_query = lax.all_gather(new_queries, 'seq', axis=2, tiled=True)  69.3 us
    all_gather x1, waiting for transfers between devices, per_device(): lax.all_gather(w_value, 'seq', axis=0, tiled=True)  61.3 us
  transfers between devices with their start and end apart: 7, of which 7 were waited for; matrix products, arithmetic and copies ran while one was open for 5% of the time, Pallas kernels for 0%

commit v1 on v0

--- a/solution.py
+++ b/solution.py
@@ -70,7 +70,8 @@
     new_queries = rotate(query_rows.reshape(shaped), positions).astype(jnp.bfloat16)
     new_keys = rotate(key_rows.reshape(shaped), positions).astype(jnp.bfloat16)
     new_values = value_rows.reshape(shaped).astype(jnp.bfloat16)
-    every_query = lax.all_gather(new_queries, "seq", axis=2, tiled=True)
+    copies = jnp.concatenate([new_queries] * lax.axis_size("seq"), axis=2)
+    every_query = lax.all_to_all(copies, "seq", 2, 2, tiled=True)
     pages_here = key_cache.shape[0]
     page_ids = seq_place * pages_here + jnp.arange(pages_here, dtype=jnp.int32)
     table_slots = jnp.arange(page_table.shape[0], dtype=jnp.int32)

time: 920 us -> 885 us (0.962)
  waiting for transfers between devices: 487 us -> 441 us
    all_gather x1 -> x0, waiting for transfers between devices: 69.3 us -> none  [per_device(): every_query = lax.all_gather(new_queries, 'seq', axis=2, tiled=True)]
    all_gather x1, waiting for transfers between devices: 61.3 us -> 82.6 us  [per_device(): lax.all_gather(w_value, 'seq', axis=0, tiled=True)]
  transfers between devices with their start and end apart: 7 -> 7, of which waited for: 7 -> 6; matrix products, arithmetic and copies ran while one was open for 5% -> 5% of each run, Pallas kernels for 0% -> 0%
where the time goes in v1:
time: 885 us; the launch traced here: 884 us
  waiting for transfers between devices  441 us (50%)
  blocking collectives  276 us (31%)
  matrix products  64.7 us (7%)
  local copies, waits for them, and re-layouts  57.9 us (7%)
  other arithmetic  20.7 us (2%)
  between operations  15.2 us (2%)
    unnamed x1, blocking collectives  140 us
    pmax x1, blocking collectives, per_device(): overall = lax.pmax(row_peak, 'seq')  136 us
    reduce_scatter x1, waiting for transfers between devices, per_device(): lax.psum_scatter(row_out * rescale[..., None], 'seq', scatter_dimension=2...  84.5 us
    all_gather x1, waiting for transfers between devices, per_device(): lax.all_gather(w_value, 'seq', axis=0, tiled=True)  82.6 us
    all_gather x1, waiting for transfers between devices, per_device(): lax.all_gather(w_out, 'seq', axis=0, tiled=True)  80.7 us
    all_gather x1, waiting for transfers between devices, per_device(): lax.all_gather(w_key, 'seq', axis=0, tiled=True)  80.2 us
    all_gather x1, waiting for transfers between devices, per_device(): lax.all_gather(w_query, 'seq', axis=0, tiled=True)  74.5 us
    reduce_scatter x1, waiting for transfers between devices, per_device(): lax.psum_scatter(partial_value, 'head', scatter_dimension=1, tiled=True)  35.8 us
  transfers between devices with their start and end apart: 7, of which 6 were waited for; matrix products, arithmetic and copies ran while one was open for 5% of the time, Pallas kernels for 0%

profile of v1, /device:TPU:2, one launch (start us, length us, event | category | flops | bytes accessed | tf_op | source)
XLA Modules:
  0.0 883.7 jit_solution(5154911389480444128)
XLA Ops:
  13.3 80.2 %all-gather.7.cloned.1.call-done = bf16[5120,384]{1,0:T(8,128)(2,1)} async-done(((bf16[160,384]{1,0:T(8,128)(2,1)}), bf16[5120,384]{1,0:T(8,128)(2,1)}) %all-gather.7.cloned.1.call-update) | async-done | bytes 3932176 | tf_op jit(solution)/shard_map/all_gather | solution.py:57
  93.4 6.3 copy.103
  99.8 74.5 %all-gather.5.cloned.1.call-done = bf16[5120,384]{1,0:T(8,128)(2,1)} async-done(((bf16[160,384]{1,0:T(8,128)(2,1)}), bf16[5120,384]{1,0:T(8,128)(2,1)}) %all-gather.5.cloned.1.call-update) | async-done | bytes 3932176 | tf_op jit(solution)/shard_map/all_gather | solution.py:56
  174.3 6.4 copy.100
  180.7 3.5 fusion.59
  187.0 3.6 copy.101
  190.6 7.3 all-to-all-start
  205.4 82.6 %all-gather.9.cloned.1.call-done = bf16[5120,384]{1,0:T(8,128)(2,1)} async-done(((bf16[160,384]{1,0:T(8,128)(2,1)}), bf16[5120,384]{1,0:T(8,128)(2,1)}) %all-gather.9.cloned.1.call-update) | async-done | bytes 3932176 | tf_op jit(solution)/shard_map/all_gather | solution.py:58
  288.0 6.3 copy.105
  295.1 4.0 convolution_convert_fusion
  299.1 82.5 %while.16 = (s32[]{:T(128)}, f32[2,8,256,3]{2,1,3,0:T(8,128)}, f32[2,8,256,3]{2,1,3,0:T(8,128)}, f32[2,8,256,3,128]{4,2,3,1,0:T(8,128)}, s32[16]{0:T(128)S(1)}, ...) while((s32[]{:T(128)}, f32[2,8,256,3]{2,1,3,0:T(8,128)}, ...), condition=%wide.region_9.10_spmd.clone.clone, body=%wide.region_3.9_spmd.clone.clone.sunk | while | flops 1071998720 | bytes 102284000 | solution.py:145
  303.9 3.7 bitcast_reduce_fusion.2
  311.1 7.6 bitcast_multiply_fusion.4
  325.9 11.2 %fusion.103 = f32[1,8,256,3,128]{4,1,3,2,0:T(8,128)S(1)} fusion(f32[8,3,128,256]{2,0,1,3:T(8,128)} %copy.163, f32[16,256,3,128]{3,1,2,0:T(8,128)} %bitcast_multiply_fusion.4, f32[8,256,3]{0,2,1:T(4,128)} %copy.164, f32[8,256,3]{0,2,1:T(4,128)} %copy.165, s32[16]{0:T(128)S(1)} %get-tuple-element.354), kind=kOutput, calls=%fused_computation.19.clone.1 | convolution fusion | flops 153354496 | bytes 12632128 | tf_op jit(solution)/shard_map/while/body/eval_jaxpr/pr,pqhd->rqhd/dot_general | solution.py:117
  345.1 3.7 bitcast_reduce_fusion.2
  352.4 7.6 bitcast_multiply_fusion.4
  367.1 11.2 %fusion.103 = f32[1,8,256,3,128]{4,1,3,2,0:T(8,128)S(1)} fusion(f32[8,3,128,256]{2,0,1,3:T(8,128)} %copy.163, f32[16,256,3,128]{3,1,2,0:T(8,128)} %bitcast_multiply_fusion.4, f32[8,256,3]{0,2,1:T(4,128)} %copy.164, f32[8,256,3]{0,2,1:T(4,128)} %copy.165, s32[16]{0:T(128)S(1)} %get-tuple-element.354), kind=kOutput, calls=%fused_computation.19.clone.1 | convolution fusion | flops 153354496 | bytes 12632128 | tf_op jit(solution)/shard_map/while/body/eval_jaxpr/pr,pqhd->rqhd/dot_general | solution.py:117
  381.6 136.1 %pmax.7 = f32[2,8,256,3]{2,1,3,0:T(8,128)S(1)} all-reduce(f32[2,8,256,3]{2,1,3,0:T(8,128)} %get-tuple-element.72), channel_id=1, replica_groups=mesh['seq'=32,'head'=8] {'seq'}, use_global_device_ids=true, to_apply=%region_10.11 | all-reduce | flops 12288 | bytes 98304 | tf_op jit(solution)/shard_map/pmax | solution.py:146
  518.6 7.2 broadcast_multiply_fusion
  527.7 140.4 %all-reduce = f32[2,8,256,3]{2,1,3,0:T(8,128)S(1)} all-reduce(f32[2,8,256,3]{2,1,3,0:T(8,128)S(1)} %get-tuple-element.213), channel_id=3, replica_groups=mesh['seq'=32,'head'=8] {'seq'}, use_global_device_ids=true, to_apply=%region_12.13.clone | all-reduce | flops 12288 | bytes 98304
  668.2 84.5 %reduce-scatter.4.cloned.1.call-done = f32[2,8,8,3,128]{4,2,3,1,0:T(8,128)} async-done(((f32[2,8,256,3,128]{4,2,3,1,0:T(8,128)}), f32[2,8,8,3,128]{4,2,3,1,0:T(8,128)}) %reduce-scatter.4.cloned.1.call-update) | async-done | bytes 196624 | tf_op jit(solution)/shard_map/reduce_scatter | solution.py:149
  753.7 80.7 %all-gather.11.cloned.1.call-done = bf16[5120,384]{1,0:T(8,128)(2,1)} async-done(((bf16[160,384]{1,0:T(8,128)(2,1)}), bf16[5120,384]{1,0:T(8,128)(2,1)}) %all-gather.11.cloned.1.call-update) | async-done | bytes 3932176 | tf_op jit(solution)/shard_map/all_gather | solution.py:59
  834.4 5.0 fusion.66
  839.4 35.8 %reduce-scatter.6.cloned.1.call-done = f32[128,640]{1,0:T(8,128)} async-done(((f32[128,5120]{1,0:T(8,128)}), f32[128,640]{1,0:T(8,128)}) %reduce-scatter.6.cloned.1.call-update) | async-done | bytes 327696 | tf_op jit(solution)/shard_map/reduce_scatter | solution.py:158
  (157 shorter events, 58.7 us)
Async XLA Ops:
  7.2 5.8 copy-start.10
  7.2 86.2 %all-gather.7.cloned.1.call-start = ((), (), s32[]{:S(2)}) async-start(), calls=%async_computation.4 | async-start | bytes 4055040 | tf_op jit(solution)/shard_map/all_gather | solution.py:57
  7.9 166.4 %all-gather.5.cloned.1.call-start = ((), (), s32[]{:S(2)}) async-start(), calls=%async_computation.3 | async-start | bytes 4055040 | tf_op jit(solution)/shard_map/all_gather | solution.py:56
  8.7 279.4 %all-gather.9.cloned.1.call-start = ((), (), s32[]{:S(2)}) async-start(), calls=%async_computation.5 | async-start | bytes 4055040 | tf_op jit(solution)/shard_map/all_gather | solution.py:58
  174.3 6.4 copy-start.2
  174.3 6.4 copy-start.9
  180.7 3.5 copy-start.1
  190.6 108.5 %all-to-all-start = ((bf16[2,8,256,3,128]{4,1,3,0,2:T(8,128)(2,1)}), bf16[2,8,256,3,128]{4,1,3,0,2:T(8,128)(2,1)}, u32[]{:S(2)}, u32[]{:S(2)}) async-start(bf16[2,8,256,3,128]{4,1,3,0,2:T(8,128)(2,1)} %copy.101), calls=%async_computation | async-start | bytes 6291456 | tf_op jit(solution)/shard_map/all_to_all | solution.py:74
  198.0 554.7 %reduce-scatter.4.cloned.1.call-start = ((), (), s32[]{:S(2)}) async-start(), calls=%async_computation.6 | async-start | bytes 6488064 | tf_op jit(solution)/shard_map/reduce_scatter | solution.py:149
  201.6 3.6 copy-start.8
  307.6 2.6 copy-start
  311.1 7.6 copy-start.3
  337.1 2.3 copy-start.6
  337.1 2.5 copy-start.4
  339.7 0.6 copy-start.7
  339.7 0.6 copy-start.5
  348.8 2.6 copy-start
  352.3 7.6 copy-start.3
  378.3 2.4 copy-start.6
  378.3 2.6 copy-start.4
  380.9 0.6 copy-start.7
  525.8 0.7 copy-start.11
  525.8 308.6 %all-gather.11.cloned.1.call-start = ((), (), s32[]{:S(2)}) async-start(), calls=%async_computation.7 | async-start | bytes 4055040 | tf_op jit(solution)/shard_map/all_gather | solution.py:59
  526.4 348.8 %reduce-scatter.6.cloned.1.call-start = ((), (), s32[]{:S(2)}) async-start(), calls=%async_computation.8 | async-start | bytes 2949120 | tf_op jit(solution)/shard_map/reduce_scatter | solution.py:158
  (1 other events, 0.6 us)
Sparse Core Ops, SparseCore 0:
  10.6 82.7 all-gather.6
  96.0 78.2 all-gather.4
  176.9 111.1 all-gather.8
  526.0 226.6 reduce-scatter.3
  755.4 78.9 all-gather.10
  839.5 35.6 reduce-scatter.5
